TPU v7x, 256 devices: a whole 4x4x8 slice. The times are simulated.
256 devices in a mesh: dev: 256 (over z, y, x, core).
Axes of the slice: x: 4, y: 4, z: 8, core: 2. Of those that a mesh axis runs over, the one named last changes fastest.
Arguments:
- left_table: float32 [524288, 256], P('dev'), may hold values from -6 to 6
- left_state: float32 [524288], P('dev'), may hold values from 0.001 to 0.1
- right_table: float32 [524288, 256], P('dev'), may hold values from -6 to 6
- right_state: float32 [524288], P('dev'), may hold values from 0.001 to 0.1
- relations: float32 [4, 256, 256], replicated, may hold values from -0.375 to 0.375
- relation_state: float32 [4, 256], replicated, may hold values from 6553 to 655360
- edge_weights: int32 [256, 4, 16, 128, 128], P('dev'), may hold values from 0 to 3
- tile_left: int32 [256, 4, 16], P('dev'), may hold values from 0 to 15
- tile_right: int32 [256, 4, 16], P('dev'), may hold values from 0 to 15
- tile_relation: int32 [256, 4, 16], P('dev'), may hold values from 0 to 3
- live_count: int32 [256, 4], P('dev'), may hold values from 2 to 16, as said below
Outputs:
- left_out: float32 [524288, 256], P('dev')
- left_state_out: float32 [524288], P('dev')
- right_out: float32 [524288, 256], P('dev')
- right_state_out: float32 [524288], P('dev')
- relations_out: float32 [4, 256, 256], replicated
- relation_state_out: float32 [4, 256], replicated
Inputs may be any that keep to these rules, and one draw needn't show every extreme that they name: `live_count`: in round 0 some partition has exactly 16 live slots.
All inputs are finite; a program needn't handle non-finite values.
Results may differ from a plain program's by a relative error of at most 0.0003.
Values sent between devices are 32-bit elements; how exact they have to be, the bound alone decides.
A program may use at most 128 MiB of HBM per device.

v0:
```python
import jax
import jax.numpy as jnp
from jax import lax
from jax.sharding import Mesh
from jax.sharding import PartitionSpec as P

D = 256
DEV = ("dev_0", "dev_1", "dev_2", "dev_3")


HIGHEST = lax.Precision.HIGHEST
learn_rate = 0.1
epsilon = 1e-06
weight_scale = 3.0


def shifted(block, axis, distance):
    devices = range(lax.axis_size(axis))
    route = [((i - distance) % len(devices), i) for i in devices]
    return lax.ppermute(block, axis, route)


def filled_up(lines, count):
    spare = -lines.shape[0] % count
    if not spare:
        return lines
    return jnp.concatenate([lines, jnp.zeros((spare, *lines.shape[1:]), lines.dtype)])


def reduced_to_own(blocks, axes, turns):
    lengths = [lax.axis_size(a) for a in axes]
    blocks = blocks.reshape(*lengths, *blocks.shape[1:])
    blocks = blocks.transpose(*turns, *range(len(axes), blocks.ndim))
    blocks = blocks.reshape(-1, *blocks.shape[len(axes) :])
    for k in turns:
        blocks = lax.psum_scatter(blocks, axes[k], scatter_dimension=0, tiled=True)
    return blocks[0]


def gather_in_order(x, axes, turns):
    blocks = x
    for k in turns:
        blocks = lax.all_gather(blocks, axes[k])
    done = turns[::-1]
    back = [done.index(k) for k in range(len(axes))]
    blocks = blocks.transpose(*back, *range(len(axes), blocks.ndim))
    return blocks.reshape(-1, *x.shape)


def sum_by_parts(x, axes, turns):
    count, lines = (lax.axis_size(axes), x.reshape(-1, *x.shape[1:][-1:]))
    blocks = filled_up(lines, count).reshape(count, -1, *lines.shape[1:])
    own = reduced_to_own(blocks, axes, turns)
    whole = gather_in_order(own, axes, turns[::-1]).reshape(-1, *lines.shape[1:])
    return whole[: len(lines)].reshape(x.shape)


def slot_terms(rows_a, rows_b, relation_map, weights, live):
    scale = D ** (-0.5)
    projected = jnp.dot(rows_a, relation_map, precision=HIGHEST)
    scores = jnp.dot(projected, rows_b.T, precision=HIGHEST) * scale
    positive = weights.astype(jnp.float32) / weight_scale
    negative = (weights == 0).astype(jnp.float32)
    dscore = (negative * jax.nn.sigmoid(scores) - positive * jax.nn.sigmoid(-scores)) * (
        live * scale
    )
    term_b = jnp.dot(dscore.T, projected, precision=HIGHEST)
    backed = jnp.dot(dscore, rows_b, precision=HIGHEST)
    term_a = jnp.dot(backed, relation_map.T, precision=HIGHEST)
    term_rel = jnp.dot(rows_a.T, backed, precision=HIGHEST)
    return (term_a, term_b, term_rel)


def bucket_grads(table_a, table_b, relations, edges, lefts, rights, kinds, count, finish):
    tile = edges.shape[-1]

    def add_slot(index, grads):
        grad_a, grad_b, grad_rel = grads
        start_a = lefts[index] * tile
        start_b = rights[index] * tile
        rows_a = lax.dynamic_slice_in_dim(table_a, start_a, tile, 0)
        rows_b = lax.dynamic_slice_in_dim(table_b, start_b, tile, 0)
        relation_map = lax.dynamic_index_in_dim(relations, kinds[index], 0, keepdims=False)
        live = (index < count).astype(jnp.float32)
        term_a, term_b, term_rel = slot_terms(rows_a, rows_b, relation_map, edges[index], live)
        grad_a = lax.dynamic_update_slice_in_dim(
            grad_a, lax.dynamic_slice_in_dim(grad_a, start_a, tile, 0) + term_a, start_a, 0
        )
        grad_b = lax.dynamic_update_slice_in_dim(
            grad_b, lax.dynamic_slice_in_dim(grad_b, start_b, tile, 0) + term_b, start_b, 0
        )
        grad_rel = grad_rel.at[kinds[index]].add(term_rel)
        return (grad_a, grad_b, grad_rel)

    start = (jnp.zeros_like(table_a), jnp.zeros_like(table_b), jnp.zeros_like(relations))
    return lax.fori_loop(jnp.int32(0), finish, add_slot, start)


def adagrad_rows(table, state, grad):
    state_new = state + jnp.mean(grad * grad, axis=1)
    table_new = table - learn_rate * grad / (jnp.sqrt(state_new)[:, None] + epsilon)
    return (table_new, state_new)


def per_device(
    left_table,
    left_state,
    right_table,
    right_state,
    relations,
    relation_state,
    edge_weights,
    tile_left,
    tile_right,
    tile_relation,
    live_count,
):
    edges = edge_weights[0]
    lefts = tile_left[0]
    rights = tile_right[0]
    kinds = tile_relation[0]
    counts = live_count[0]
    rounds = edges.shape[0]
    active = edges.shape[1]
    bounds = jnp.full((rounds,), active, jnp.int32)
    rel_grad = jnp.zeros_like(relations)
    table_left, state_left = (left_table, left_state)
    table_right, state_right = (right_table, right_state)
    for turn in range(rounds):
        grad_a, grad_b, grad_rel = bucket_grads(
            table_left,
            table_right,
            relations,
            edges[turn],
            lefts[turn],
            rights[turn],
            kinds[turn],
            counts[turn],
            bounds[turn],
        )
        rel_grad = rel_grad + grad_rel
        table_left, state_left = adagrad_rows(table_left, state_left, grad_a)
        table_right, state_right = adagrad_rows(table_right, state_right, grad_b)
        if turn + 1 < rounds:
            table_right, state_right = shifted((table_right, state_right), DEV, 1)
    table_right, state_right = shifted((table_right, state_right), DEV, -(rounds - 1))
    kinds_count, width = (relations.shape[0], relations.shape[1])
    flat_grad = rel_grad.reshape(kinds_count * width, width)
    flat_rel = relations.reshape(kinds_count * width, width)
    flat_state = relation_state.reshape(kinds_count * width)
    total = sum_by_parts(flat_grad, DEV, (3, 0, 1, 2))
    new_rel, new_state = adagrad_rows(flat_rel, flat_state, total)
    return (
        table_left,
        state_left,
        table_right,
        state_right,
        new_rel.reshape(kinds_count, width, width),
        new_state.reshape(kinds_count, width),
    )


def solution(mesh):
    torus = Mesh(mesh.devices.reshape(8, 4, 4, 2), ("dev_0", "dev_1", "dev_2", "dev_3"))
    return jax.shard_map(
        per_device,
        mesh=torus,
        in_specs=(
            P(DEV, None),
            P(DEV),
            P(DEV, None),
            P(DEV),
            P(),
            P(),
            P(DEV, None, None, None, None),
            P(DEV, None, None),
            P(DEV, None, None),
            P(DEV, None, None),
            P(DEV, None),
        ),
        out_specs=(P(DEV, None), P(DEV), P(DEV, None), P(DEV), P(), P()),
        check_vma=False,
    )
```

profile of v0, /device:TPU:58, one launch (start us, length us, event | category | flops | bytes accessed | tf_op | source)
XLA Modules:
  0.0 1352.8 jit_solution(14104536419784989877)
XLA Ops:
  7.3 4.3 slice_bitcast_fusion
  14.9 234.2 %while.60 = (s32[]{:T(128)}, f32[2048,256]{1,0:T(8,128)S(1)}, f32[2048,256]{1,0:T(8,128)}, f32[4,256,256]{2,1,0:T(8,128)}, s32[16]{0:T(128)S(1)}, /*index=5*/s32...) while((s32[]{:T(128)}, f32[2048,256]{1,0:T(8,128)S(1)}, ...), condition=%wide.region_2.3_spmd, body=%wide.region_0.2_spmd.sunk | while | flops 453394464 | bytes 3148202 | solution.py:96
  251.3 3.4 divide_subtract_fusion.6
  259.5 20.9 %collective-permute-done = f32[2048,256]{1,0:T(8,128)} collective-permute-done((f32[2048,256]{1,0:T(8,128)}, f32[2048,256]{1,0:T(8,128)}, u32[]{:S(2)}, u32[]{:S(2)}) %collective-permute-start) | collective-permute-done | bytes 2097184 | tf_op jit(solution)/shard_map/ppermute | solution.py:20
  283.1 238.4 %while.61 = (s32[]{:T(128)}, f32[2048,256]{1,0:T(8,128)S(1)}, f32[2048,256]{1,0:T(8,128)}, f32[4,256,256]{2,1,0:T(8,128)}, s32[16]{0:T(128)S(1)}, /*index=5*/s32...) while((s32[]{:T(128)}, f32[2048,256]{1,0:T(8,128)S(1)}, ...), condition=%wide.region_7.8_spmd, body=%wide.region_5.7_spmd.sunk | while | flops 453394464 | bytes 3148202 | solution.py:96
  523.7 3.4 divide_subtract_fusion.4
  530.7 22.2 %collective-permute-done.2 = f32[2048,256]{1,0:T(8,128)} collective-permute-done((f32[2048,256]{1,0:T(8,128)}, f32[2048,256]{1,0:T(8,128)}, u32[]{:S(2)}, u32[]{:S(2)}) %collective-permute-start.2) | collective-permute-done | bytes 2097184 | tf_op jit(solution)/shard_map/ppermute | solution.py:20
  555.5 240.5 %while.62 = (s32[]{:T(128)}, f32[2048,256]{1,0:T(8,128)S(1)}, f32[2048,256]{1,0:T(8,128)}, f32[4,256,256]{2,1,0:T(8,128)}, s32[16]{0:T(128)S(1)}, /*index=5*/s32...) while((s32[]{:T(128)}, f32[2048,256]{1,0:T(8,128)S(1)}, ...), condition=%wide.region_12.13_spmd, body=%wide.region_10.12_spmd.sunk | while | flops 453394464 | bytes 3148202 | solution.py:96
  798.2 3.4 divide_subtract_fusion.2
  804.9 22.5 %collective-permute-done.4 = f32[2048,256]{1,0:T(8,128)} collective-permute-done((f32[2048,256]{1,0:T(8,128)}, f32[2048,256]{1,0:T(8,128)}, u32[]{:S(2)}, u32[]{:S(2)}) %collective-permute-start.4) | collective-permute-done | bytes 2097184 | tf_op jit(solution)/shard_map/ppermute | solution.py:20
  830.0 244.0 %while.63 = (s32[]{:T(128)}, f32[2048,256]{1,0:T(8,128)S(1)}, f32[2048,256]{1,0:T(8,128)}, f32[4,256,256]{2,1,0:T(8,128)}, s32[16]{0:T(128)S(1)}, /*index=5*/s32...) while((s32[]{:T(128)}, f32[2048,256]{1,0:T(8,128)S(1)}, ...), condition=%wide.region_17.18_spmd, body=%wide.region_15.17_spmd.sunk | while | flops 453394464 | bytes 3148202 | solution.py:96
  842.5 2.8 fusion.265
  857.7 2.8 fusion.265
  1074.0 3.4 add_add_fusion
  1087.0 39.6 %all-reduce.8.cloned.1.call-done = f32[256,4,256]{2,1,0:T(4,128)} async-done(((f32[256,4,256]{2,1,0:T(4,128)}), f32[256,4,256]{2,1,0:T(4,128)}) %all-reduce.8.cloned.1.call-update) | async-done | bytes 1048592
  1128.5 3.9 divide_subtract_fusion
  1135.9 68.4 %all-reduce.10.cloned.1.call-done = f32[128,4,256]{2,1,0:T(4,128)} async-done(((f32[128,4,256]{2,1,0:T(4,128)}), f32[128,4,256]{2,1,0:T(4,128)}) %all-reduce.10.cloned.1.call-update) | async-done | bytes 524304
  1207.6 43.2 %all-reduce.12.cloned.1.call-done = f32[16,4,256]{2,1,0:T(4,128)} async-done(((f32[16,4,256]{2,1,0:T(4,128)}), f32[16,4,256]{2,1,0:T(4,128)}) %all-reduce.12.cloned.1.call-update) | async-done | bytes 65552
  1251.6 13.9 %all-reduce.3 = f32[4,4,256]{2,1,0:T(4,128)S(1)} all-reduce(f32[4,4,256]{2,1,0:T(4,128)S(1)} %constant_dynamic-slice_fusion.1), channel_id=8, replica_groups=mesh['dev_0'=8,'dev_1'=4,'dev_2'=4,'dev_3'=2] {'dev_2'}, use_global_device_ids=true, to_apply=%region_23.24.clone | all-reduce | flops 4096 | bytes 32768
  1266.1 12.3 all_gather.21
  1278.4 11.8 all-gather
  1290.2 27.8 %all-gather.1 = f32[32,4,4,256]{3,2,1,0:T(4,128)} all-gather(f32[4,4,4,256]{3,2,1,0:T(4,128)S(1)} %bitcast.298), channel_id=3, replica_groups=mesh['dev_0'=8,'dev_1'=4,'dev_2'=4,'dev_3'=2] {'dev_0'}, dimensions={0}, use_global_device_ids=true | all-gather | bytes 589824 | tf_op jit(solution)/shard_map/all_gather | solution.py:43
  1321.5 12.9 all-gather.5.cloned.1.call-done
  1342.6 3.0 copy.105
  (758 shorter events, 767.5 us)
Async XLA Ops:
  7.2 4.4 copy-start.11
  7.2 5.0 copy-start.14
  7.2 5.0 copy-start.15
  7.2 5.0 copy-start.16
  7.2 1119.3 %all-reduce.8.cloned.1.call-start = ((), (), s32[]{:S(2)}) async-start(), calls=%async_computation.1 | async-start | bytes 2097152
  12.3 2.6 copy-start
  12.4 2.6 copy-start.9
  254.7 25.8 %collective-permute-start = (f32[2048,256]{1,0:T(8,128)}, f32[2048,256]{1,0:T(8,128)}, u32[]{:S(2)}, u32[]{:S(2)}) collective-permute-start(f32[2048,256]{1,0:T(8,128)} %divide_subtract_fusion.6), channel_id=1, source_target_pairs={{255,0},{0,1},{1,2},{2,3},{3,4},{4,5},{5,6},{6,7},{7,8},{8,9},{9,1... | collective-permute-start | bytes 6291464 | tf_op jit(solution)/shard_map/ppermute | solution.py:20
  254.7 268.9 %collective-permute-start.1 = (f32[2048]{0:T(1024)S(1)}, f32[2048]{0:T(1024)S(1)}, u32[]{:S(2)}, u32[]{:S(2)}) collective-permute-start(f32[2048]{0:T(1024)S(1)} %get-tuple-element.431), channel_id=1, source_target_pairs={{255,0},{0,1},{1,2},{2,3},{3,4},{4,5},{5,6},{6,7},{7,8},{8,9},{9,1... | collective-permute-start | bytes 24584 | tf_op jit(solution)/shard_map/ppermute | solution.py:20
  527.1 25.8 %collective-permute-start.2 = (f32[2048,256]{1,0:T(8,128)}, f32[2048,256]{1,0:T(8,128)}, u32[]{:S(2)}, u32[]{:S(2)}) collective-permute-start(f32[2048,256]{1,0:T(8,128)} %divide_subtract_fusion.4), channel_id=1, source_target_pairs={{255,0},{0,1},{1,2},{2,3},{3,4},{4,5},{5,6},{6,7},{7,8},{8,9},{9,1... | collective-permute-start | bytes 6291464 | tf_op jit(solution)/shard_map/ppermute | solution.py:20
  527.1 271.0 %collective-permute-start.3 = (f32[2048]{0:T(1024)S(1)}, f32[2048]{0:T(1024)S(1)}, u32[]{:S(2)}, u32[]{:S(2)}) collective-permute-start(f32[2048]{0:T(1024)S(1)} %get-tuple-element.427), channel_id=1, source_target_pairs={{255,0},{0,1},{1,2},{2,3},{3,4},{4,5},{5,6},{6,7},{7,8},{8,9},{9,1... | collective-permute-start | bytes 24584 | tf_op jit(solution)/shard_map/ppermute | solution.py:20
  801.6 25.8 %collective-permute-start.4 = (f32[2048,256]{1,0:T(8,128)}, f32[2048,256]{1,0:T(8,128)}, u32[]{:S(2)}, u32[]{:S(2)}) collective-permute-start(f32[2048,256]{1,0:T(8,128)} %divide_subtract_fusion.2), channel_id=1, source_target_pairs={{255,0},{0,1},{1,2},{2,3},{3,4},{4,5},{5,6},{6,7},{7,8},{8,9},{9,1... | collective-permute-start | bytes 6291464 | tf_op jit(solution)/shard_map/ppermute | solution.py:20
  1080.0 2.6 copy-start.20
  1082.5 121.7 %all-reduce.10.cloned.1.call-start = ((), (), s32[]{:S(2)}) async-start(), calls=%async_computation.2 | async-start | bytes 1048576
  1083.8 3.2 collective-permute-start.5
  1128.4 122.4 %all-reduce.12.cloned.1.call-start = ((), (), s32[]{:S(2)}) async-start(), calls=%async_computation.3 | async-start | bytes 131072
  1128.5 6.2 copy-start.19
  1128.5 77.3 %copy-start.18 = (u32[256]{0:T(256)S(1)}, u32[256]{0:T(256)}, u32[]{:S(2)}) copy-start(u32[256]{0:T(256)} %constant.253) | copy-start | bytes 3076
  1128.5 77.9 %copy-start.17 = (u32[256]{0:T(256)S(1)}, u32[256]{0:T(256)}, u32[]{:S(2)}) copy-start(u32[256]{0:T(256)} %constant.257) | copy-start | bytes 3076
  1132.4 189.1 %collective-permute-start.6 = (f32[2048,256]{1,0:T(8,128)}, f32[2048,256]{1,0:T(8,128)}, u32[]{:S(2)}, u32[]{:S(2)}) collective-permute-start(f32[2048,256]{1,0:T(8,128)} %divide_subtract_fusion), channel_id=1, source_target_pairs={{3,0},{4,1},{5,2},{6,3},{7,4},{8,5},{9,6},{10,7},{11,8},{12,9},{13... | collective-permute-start | bytes 6291464 | tf_op jit(solution)/shard_map/ppermute | solution.py:20
  1205.8 128.6 %all-gather.5.cloned.1.call-start = ((), (), s32[]{:S(2)}) async-start(), calls=%async_computation | async-start | bytes 1572864 | tf_op jit(solution)/shard_map/all_gather | solution.py:43
  1318.1 3.4 collective-permute-start.7
  1336.3 3.3 copy-start.8
  1338.0 2.9 copy-start.13
  (9 other events, 17.4 us)
Sparse Core Ops, SparseCore 0:
  1082.6 43.8 all-reduce.7
  1129.4 74.7 all-reduce.9
  1207.1 43.6 all-reduce.11
  1318.2 16.1 all-gather.4
where the time goes:
time: 1370 us; the launch traced here: 1350 us
  matrix products  552 us (40%)
  loops' own time  243 us (18%)
  waiting for transfers between devices  231 us (17%)
  local copies, waits for them, and re-layouts  154 us (11%)
  other arithmetic  85.1 us (6%)
  blocking collectives  65.8 us (5%)
  between operations  16.1 us (1%)
    another operation x4, loops' own time, bucket_grads(): return lax.fori_loop(jnp.int32(0), finish, add_slot, start)  243 us
    dot_general x64, matrix products, slot_terms(): term_rel = jnp.dot(rows_a.T, backed, precision=HIGHEST)  177 us
    unnamed x7, waiting for transfers between devices  151 us
    dot_general x64, matrix products, slot_terms(): term_b = jnp.dot(dscore.T, projected, precision=HIGHEST)  120 us
    dot_general x64, matrix products, slot_terms(): scores = jnp.dot(projected, rows_b.T, precision=HIGHEST) * scale  77.7 us
    dot_general x64, matrix products, slot_terms(): projected = jnp.dot(rows_a, relation_map, precision=HIGHEST)  76.2 us
    dot_general x64, matrix products, slot_terms(): backed = jnp.dot(dscore, rows_b, precision=HIGHEST)  74.4 us
    ppermute x8, waiting for transfers between devices, shifted(): return lax.ppermute(block, axis, route)  66.8 us
  transfers between devices with their start and end apart: 12, of which 9 were waited for; matrix products, arithmetic and copies ran while one was open for 28% of the time, Pallas kernels for 0%

commit v1 on v0

v1 whole, which is shorter than its diff:
```python
import functools
import jax
import jax.numpy as jnp
from jax import lax
from jax.experimental import pallas as pl
from jax.experimental.pallas import tpu as pltpu
from jax.sharding import Mesh
from jax.sharding import PartitionSpec as P

D = 256
TILE = 128
TILES = 16
ACTIVE = 16
RELS = 4
LEARN = 0.1
EPS = 1e-6
DEV = ("dev_0", "dev_1", "dev_2", "dev_3")
F32 = jnp.float32
BF16 = jnp.bfloat16


def halves(x):
    hi = x.astype(BF16)
    lo = (x - hi.astype(F32)).astype(BF16)
    return hi, lo


def product(a, b, dims):
    (ah, al), (bh, bl) = a, b
    (ca,), (cb,) = dims
    lhs = jnp.concatenate([ah, ah, al], axis=ca)
    rhs = jnp.concatenate([bh, bl, bh], axis=cb)
    return lax.dot_general(lhs, rhs, (dims, ((), ())), preferred_element_type=F32)


NN = ((1,), (0,))
NT = ((1,), (1,))


def round_kernel(
    turn,
    chained,
    lefts,
    rights,
    kinds,
    counts,
    lstate,
    rstate,
    left_in,
    right_in,
    relations,
    edges,
    *rest,
):
    if chained:
        rel_in, *rest = rest
    (
        left_out,
        lstate_out,
        right_out,
        rstate_out,
        rel_out,
        tl,
        tr,
        gl,
        gr,
        rg,
        mf,
        mh,
        ml,
        ew,
        hitl,
        hitr,
        tsem,
        esem,
        msem,
        rsem,
        osem,
    ) = rest
    count = counts[turn]
    pairs = lax.div(count + 1, 2)
    rel_load = pltpu.make_async_copy(relations, mf, msem.at[0])
    rel_load.start()
    left_load = pltpu.make_async_copy(left_in, tl, tsem.at[0])
    right_load = pltpu.make_async_copy(right_in, tr, tsem.at[1])
    left_load.start()
    right_load.start()

    def edge_copy(s):
        return pltpu.make_async_copy(edges.at[turn, s], ew.at[s], esem.at[s])

    def edge_start(s, _):
        edge_copy(s).start()
        return 0

    lax.fori_loop(0, 2 * pairs, edge_start, 0)
    if chained:
        rg_load = pltpu.make_async_copy(rel_in, rg, rsem.at[0])
        rg_load.start()
    else:
        rg[...] = jnp.zeros_like(rg)

    def clear(t, _):
        hitl[t] = 0
        hitr[t] = 0
        rows = pl.ds(t * TILE, TILE)
        gl[rows, :] = jnp.zeros((TILE, D), F32)
        gr[rows, :] = jnp.zeros((TILE, D), F32)
        return 0

    lax.fori_loop(0, TILES, clear, 0)

    def mark(s, _):
        hitl[lefts[turn, s]] = 1
        hitr[rights[turn, s]] = 1
        return 0

    lax.fori_loop(0, count, mark, 0)
    rel_load.wait()

    def split(r, _):
        hi, lo = halves(mf[r])
        mh[r] = hi
        ml[r] = lo
        return 0

    lax.fori_loop(0, RELS, split, 0)
    left_load.wait()
    right_load.wait()

    def out_copy(side, t):
        src, dst = ((tl, left_out), (tr, right_out))[side]
        rows = pl.ds(t * TILE, TILE)
        return pltpu.make_async_copy(src.at[rows, :], dst.at[rows, :], osem.at[side, t])

    def early(t, _):
        for side, hit in ((0, hitl), (1, hitr)):

            @pl.when(hit[t] == 0)
            def _():
                out_copy(side, t).start()

        return 0

    lax.fori_loop(0, TILES, early, 0)
    if chained:
        rg_load.wait()

    def pair(i, _):
        slots = (2 * i, 2 * i + 1)
        for s in slots:
            edge_copy(s).wait()
        at = [lefts[turn, s] * TILE for s in slots]
        bt = [rights[turn, s] * TILE for s in slots]
        kd = [kinds[turn, s] for s in slots]
        live = [jnp.where(s < count, 1.0, 0.0).astype(F32) for s in slots]
        af = [tl[pl.ds(a, TILE), :] for a in at]
        a = [halves(x) for x in af]
        m = [(mh[k], ml[k]) for k in kd]
        p = [halves(product(x, y, NN)) for x, y in zip(a, m)]
        b = [halves(tr[pl.ds(x, TILE), :]) for x in bt]
        s_ = [product(x, y, NT) for x, y in zip(p, b)]
        g = []
        for s, sc, lv in zip(slots, s_, live):
            w = ew[s]
            zero = w == 0
            sc = sc * (D**-0.5)
            sig = jax.nn.sigmoid(jnp.where(zero, sc, -sc))
            coef = jnp.where(zero, 1.0, w.astype(F32) * (-1.0 / 3.0))
            g.append(sig * coef * (lv * D**-0.5))
        gs = [halves(x) for x in g]
        gts = [halves(x.T) for x in g]
        backed = [halves(product(x, y, NN)) for x, y in zip(gs, b)]
        tb = [product(x, y, NN) for x, y in zip(gts, p)]
        ta = [product(x, y, NT) for x, y in zip(backed, m)]
        ats = [halves(x.T) for x in af]
        tm = [product(x, y, NN) for x, y in zip(ats, backed)]
        for j in range(2):
            rows = pl.ds(bt[j], TILE)
            gr[rows, :] += tb[j]
        for j in range(2):
            rows = pl.ds(at[j], TILE)
            gl[rows, :] += ta[j]
        for j in range(2):
            rg[kd[j]] += tm[j]
        return 0

    lax.fori_loop(0, pairs, pair, 0)
    rg_store = pltpu.make_async_copy(rg, rel_out, rsem.at[1])
    rg_store.start()
    lstate_out[...] = lstate[...]
    rstate_out[...] = rstate[...]

    def update(side, t):
        tab, grad, st, st_out = ((tl, gl, lstate, lstate_out), (tr, gr, rstate, rstate_out))[side]
        rows = pl.ds(t * TILE, TILE)
        g = grad[rows, :]
        mean = jnp.sum(g * g, axis=1, keepdims=True) * (1.0 / D)
        row = st[pl.ds(t, 1), :]
        wide = jnp.broadcast_to(row, (TILE, TILE)).T + mean
        st_out[pl.ds(t, 1), :] = wide.T[0:1, :]
        step = LEARN / (jnp.sqrt(wide) + EPS)
        tab[rows, :] = tab[rows, :] - g * jnp.concatenate([step, step], axis=1)

    def finish(t, _):
        before = jnp.maximum(t - 1, 0)
        for side, hit in ((0, hitl), (1, hitr)):

            @pl.when((t < TILES) & (hit[jnp.minimum(t, TILES - 1)] != 0))
            def _():
                update(side, t)

            @pl.when((t > 0) & (hit[before] != 0))
            def _():
                out_copy(side, before).start()

        return 0

    lax.fori_loop(0, TILES + 1, finish, 0)

    def drain(t, _):
        out_copy(0, t).wait()
        out_copy(1, t).wait()
        return 0

    lax.fori_loop(0, TILES, drain, 0)
    rg_store.wait()


def run_round(turn, ids, left, lstate, right, rstate, relations, edges, rel_grad):
    smem = pl.BlockSpec(memory_space=pltpu.SMEM)
    vmem = pl.BlockSpec(memory_space=pltpu.VMEM)
    hbm = pl.BlockSpec(memory_space=pl.ANY)
    rows = TILES * TILE
    args = (*ids, lstate, rstate, left, right, relations, edges)
    specs = [smem] * 4 + [vmem] * 2 + [hbm] * 4
    if rel_grad is not None:
        args += (rel_grad,)
        specs += [hbm]
    return pl.pallas_call(
        functools.partial(round_kernel, turn, rel_grad is not None),
        name="bucket_round",
        out_shape=(
            jax.ShapeDtypeStruct((rows, D), F32),
            jax.ShapeDtypeStruct((TILES, TILE), F32),
            jax.ShapeDtypeStruct((rows, D), F32),
            jax.ShapeDtypeStruct((TILES, TILE), F32),
            jax.ShapeDtypeStruct((RELS, D, D), F32),
        ),
        in_specs=specs,
        out_specs=(hbm, vmem, hbm, vmem, hbm),
        scratch_shapes=[
            pltpu.VMEM((rows, D), F32),
            pltpu.VMEM((rows, D), F32),
            pltpu.VMEM((rows, D), F32),
            pltpu.VMEM((rows, D), F32),
            pltpu.VMEM((RELS, D, D), F32),
            pltpu.VMEM((RELS, D, D), F32),
            pltpu.VMEM((RELS, D, D), BF16),
            pltpu.VMEM((RELS, D, D), BF16),
            pltpu.VMEM((ACTIVE, TILE, TILE), jnp.int32),
            pltpu.SMEM((TILES,), jnp.int32),
            pltpu.SMEM((TILES,), jnp.int32),
            pltpu.SemaphoreType.DMA((2,)),
            pltpu.SemaphoreType.DMA((ACTIVE,)),
            pltpu.SemaphoreType.DMA((1,)),
            pltpu.SemaphoreType.DMA((2,)),
            pltpu.SemaphoreType.DMA((2, TILES)),
        ],
        compiler_params=pltpu.CompilerParams(vmem_limit_bytes=62 << 20),
        cost_estimate=pl.CostEstimate(
            flops=2_400_000_000, bytes_accessed=12_000_000, transcendentals=262144
        ),
    )(*args)


AXES = (("dev_0", 8), ("dev_1", 4), ("dev_2", 4), ("dev_3", 2))
FIRST = 6 * 128
MESH = pl.DeviceIdType.MESH


def coordinates(index):
    z = lax.rem(lax.div(index, 32), 8)
    y = lax.rem(lax.div(index, 8), 4)
    x = lax.rem(lax.div(index, 2), 4)
    return (z, y, x, lax.rem(index, 2))


def home_kernel(
    back_left,
    back_right,
    left,
    lstate,
    right,
    rstate,
    grad,
    rel,
    rel_state,
    left_out,
    lstate_out,
    right_out,
    rstate_out,
    rel_out,
    rel_state_out,
    cbuf,
    yacc,
    ybuf,
    zacc,
    zbuf,
    xbuf,
    full,
    home_send,
    home_recv,
    csend,
    crecv,
    ysend,
    yrecv,
    zsend,
    zrecv,
    xsend,
    xrecv,
):
    z, y, x, c = (lax.axis_index(name) for name, _ in AXES)
    me = ((z * 4 + y) * 4 + x) * 2 + c
    count = 256

    def shifted_id(distance):
        return coordinates(lax.rem(me + count + distance, count))

    far = [(lax.rem(z + d, 8), y, x, c) for d in range(1, 8)]
    side = [(z, lax.rem(y + d, 4), x, c) for d in range(1, 4)]
    row = [(z, y, lax.rem(x + d, 4), c) for d in range(1, 4)]
    mate = (z, y, x, 1 - c)
    lines = [shifted_id(d) for d in (back_left, -back_left, back_right, -back_right)]
    peers = lines + [mate] + far + side + row
    barrier = pltpu.get_barrier_semaphore()
    for peer in peers:
        pl.semaphore_signal(barrier, inc=1, device_id=peer, device_id_type=MESH)
    pl.semaphore_wait(barrier, len(peers))

    def send(src, dst, ssem, rsem, peer):
        copy = pltpu.make_async_remote_copy(
            src_ref=src,
            dst_ref=dst,
            send_sem=ssem,
            recv_sem=rsem,
            device_id=peer,
            device_id_type=MESH,
        )
        copy.start()
        return copy

    half = 512
    copies = [
        send(
            grad.at[pl.ds((1 - c) * half, half), :], cbuf, csend.at[0], crecv.at[0], mate
        )
    ]
    homes = [
        send(rstate, rstate_out, home_send.at[0], home_recv.at[0], lines[2]),
        send(lstate, lstate_out, home_send.at[1], home_recv.at[1], lines[0]),
    ]

    def send_home(part, start, length):
        rows = pl.ds(start, length)
        for i, (src, dst, peer) in enumerate(
            ((right, right_out, lines[2]), (left, left_out, lines[0]))
        ):
            at = 2 + 2 * part + i
            homes.append(
                send(src.at[rows, :], dst.at[rows, :], home_send.at[at], home_recv.at[at], peer)
            )

    copies[0].wait()

    def add_core(i, _):
        rows = pl.ds(i * TILE, TILE)
        yacc[i] = grad[pl.ds(c * half + i * TILE, TILE), :] + cbuf[rows, :]
        return 0

    lax.fori_loop(0, 4, add_core, 0)
    copies = [
        send(yacc.at[peer[1]], ybuf.at[d], ysend.at[d], yrecv.at[d], peer)
        for d, peer in enumerate(side)
    ]
    send_home(0, 0, FIRST)
    for copy in copies:
        copy.wait()

    def add_side(i, _):
        rows = pl.ds(i * 16, 16)
        zacc[i] = (yacc[y, rows, :] + ybuf[0, rows, :]) + (ybuf[1, rows, :] + ybuf[2, rows, :])
        return 0

    lax.fori_loop(0, 8, add_side, 0)
    copies = [
        send(zacc.at[peer[0]], zbuf.at[d], zsend.at[d], zrecv.at[d], peer)
        for d, peer in enumerate(far)
    ]
    for copy in copies:
        copy.wait()
    own = zacc[z]
    for d in range(7):
        own = own + zbuf[d]
    xbuf[x] = own
    copies = [
        send(xbuf.at[x], xbuf.at[x], xsend.at[d], xrecv.at[d], peer) for d, peer in enumerate(row)
    ]
    for copy in copies:
        copy.wait()
    full[c, y, z] = (xbuf[0] + xbuf[1]) + (xbuf[2] + xbuf[3])
    piece = full.at[c, y, z]
    copies = [
        send(piece, piece, zsend.at[7 + d], zrecv.at[7 + d], peer) for d, peer in enumerate(far)
    ]
    for copy in copies:
        copy.wait()
    piece = full.at[c, y]
    copies = [
        send(piece, piece, ysend.at[3 + d], yrecv.at[3 + d], peer) for d, peer in enumerate(side)
    ]
    send_home(1, FIRST, left.shape[0] - FIRST)
    for copy in copies:
        copy.wait()
    piece = full.at[c]
    send(piece, piece, csend.at[1], crecv.at[1], mate).wait()

    def update(t, _):
        rows = pl.ds(t * TILE, TILE)
        g = full[lax.div(t, 4), lax.rem(t, 4)].reshape(TILE, D)
        mean = jnp.sum(g * g, axis=1, keepdims=True) * (1.0 / D)
        wide = jnp.broadcast_to(rel_state[pl.ds(t, 1), :], (TILE, TILE)).T + mean
        rel_state_out[pl.ds(t, 1), :] = wide.T[0:1, :]
        step = LEARN / (jnp.sqrt(wide) + EPS)
        rel_out[rows, :] = rel[rows, :] - g * jnp.concatenate([step, step], axis=1)
        return 0

    lax.fori_loop(0, 8, update, 0)
    for copy in homes:
        copy.wait()


def bring_home(back_left, back_right, left, lstate, right, rstate, grad, rel, rel_state):
    vmem = pl.BlockSpec(memory_space=pltpu.VMEM)
    hbm = pl.BlockSpec(memory_space=pl.ANY)
    like = lambda a: jax.ShapeDtypeStruct(a.shape, a.dtype)
    dma = pltpu.SemaphoreType.DMA
    return pl.pallas_call(
        functools.partial(home_kernel, back_left, back_right),
        name="bring_home",
        out_shape=tuple(like(a) for a in (left, lstate, right, rstate, rel, rel_state)),
        in_specs=[hbm] * 4 + [vmem] * 3,
        out_specs=(hbm,) * 4 + (vmem,) * 2,
        scratch_shapes=[
            pltpu.VMEM((512, D), F32),
            pltpu.VMEM((4, TILE, D), F32),
            pltpu.VMEM((3, TILE, D), F32),
            pltpu.VMEM((8, 16, D), F32),
            pltpu.VMEM((7, 16, D), F32),
            pltpu.VMEM((4, 16, D), F32),
            pltpu.VMEM((2, 4, 8, 16, D), F32),
            dma((6,)),
            dma((6,)),
            dma((2,)),
            dma((2,)),
            dma((6,)),
            dma((6,)),
            dma((14,)),
            dma((14,)),
            dma((3,)),
            dma((3,)),
        ],
        compiler_params=pltpu.CompilerParams(
            collective_id=0, has_side_effects=True, vmem_limit_bytes=62 << 20
        ),
        cost_estimate=pl.CostEstimate(
            flops=2_000_000, bytes_accessed=12_000_000, transcendentals=1024
        ),
    )(left, lstate, right, rstate, grad, rel, rel_state)


def shifted(block, axis, distance):
    devices = range(lax.axis_size(axis))
    route = [((i - distance) % len(devices), i) for i in devices]
    return lax.ppermute(block, axis, route)


def per_device(
    left_table,
    left_state,
    right_table,
    right_state,
    relations,
    relation_state,
    edge_weights,
    tile_left,
    tile_right,
    tile_relation,
    live_count,
):
    edges = edge_weights[0]
    ids = (tile_left[0], tile_right[0], tile_relation[0], live_count[0])
    rounds = edges.shape[0]
    last = rounds - 1
    packed = jnp.concatenate([x[last].reshape(-1) for x in ids])
    last_edges, packed = shifted((edges[last:], packed), DEV, -1)
    rel_grad = None
    table_left, state_left = left_table, left_state.reshape(TILES, TILE)
    table_right, state_right = right_table, right_state.reshape(TILES, TILE)
    for turn in range(last):
        table_left, state_left, table_right, state_right, rel_grad = run_round(
            turn, ids, table_left, state_left, table_right, state_right, relations, edges, rel_grad
        )
        if turn + 1 < last:
            table_right, state_right = shifted((table_right, state_right), DEV, 1)
        if turn == 0:
            table_right, last_edges, packed = lax.optimization_barrier(
                (table_right, last_edges, packed)
            )
    last_ids = [packed[i * ACTIVE : (i + 1) * ACTIVE].reshape(1, ACTIVE) for i in range(3)]
    last_ids.append(packed[3 * ACTIVE :])
    table_left, state_left = shifted((table_left, state_left), DEV, -1)
    table_left, state_left, table_right, state_right, rel_grad = run_round(
        0, last_ids, table_left, state_left, table_right, state_right, relations, last_edges, rel_grad
    )
    kinds_count, width = (relations.shape[0], relations.shape[1])
    table_left, state_left, table_right, state_right, new_rel, new_state = bring_home(
        1,
        1 - last,
        table_left,
        state_left,
        table_right,
        state_right,
        rel_grad.reshape(kinds_count * width, width),
        relations.reshape(kinds_count * width, width),
        relation_state.reshape(-1, TILE),
    )
    return (
        table_left,
        state_left.reshape(-1),
        table_right,
        state_right.reshape(-1),
        new_rel.reshape(kinds_count, width, width),
        new_state.reshape(kinds_count, width),
    )


def solution(mesh):
    torus = Mesh(mesh.devices.reshape(8, 4, 4, 2), ("dev_0", "dev_1", "dev_2", "dev_3"))
    return jax.shard_map(
        per_device,
        mesh=torus,
        in_specs=(
            P(DEV, None),
            P(DEV),
            P(DEV, None),
            P(DEV),
            P(),
            P(),
            P(DEV, None, None, None, None),
            P(DEV, None, None),
            P(DEV, None, None),
            P(DEV, None, None),
            P(DEV, None),
        ),
        out_specs=(P(DEV, None), P(DEV), P(DEV, None), P(DEV), P(), P()),
        check_vma=False,
    )
```

time: 1370 us -> 236 us (0.17)
  the two profiles are of different devices: /device:TPU:58 before, /device:TPU:15 now
where the time goes in v1:
time: 236 us; the launch traced here: 239 us
  Pallas kernels  140 us (59%)
  waiting for transfers between devices  57.8 us (24%)
  starting transfers between devices  24.7 us (10%)
  local copies, waits for them, and re-layouts  15 us (6%)
    pallas_call x1, Pallas kernels, bring_home(): pl.pallas_call(functools.partial(home_kernel, back_left, back_right), nam...  104 us
    ppermute x8, waiting for transfers between devices, shifted(): return lax.ppermute(block, axis, route)  57.8 us
    pallas_call x4, Pallas kernels, run_round(): pl.pallas_call(functools.partial(round_kernel, turn, rel_grad is not None...  35.8 us
    ppermute x8, starting transfers between devices, shifted(): return lax.ppermute(block, axis, route)  24.7 us
    unnamed x27, local copies, waits for them, and re-layouts  8.57 us
  transfers between devices with their start and end apart: 8, of which 4 were waited for; matrix products, arithmetic and copies ran while one was open for 2% of the time, Pallas kernels for 0%

profile of v1, /device:TPU:15, one launch (start us, length us, event | category | flops | bytes accessed | tf_op | source)
XLA Modules:
  0.0 238.5 jit_solution(4709417536154132083)
XLA Ops:
  0.6 7.2 %bucket_round.4 = (f32[2048,256]{1,0:T(8,128)}, f32[16,128]{1,0:T(8,128)}, f32[2048,256]{1,0:T(8,128)}, f32[16,128]{1,0:T(8,128)}, f32[4,256,256]{2,1,0:T(8,128)}) custom-call(s32[4,16]{1,0:T(4,128)} %bitcast.39, s32[4,16]{1,0:T(4,128)} %bitcast.36, s32[4,16]{1,0:T(4,128)} %bitcast.33, s32[4]{0:T(128)} %bitcast.46, f32[16,128]{1,0:T(8,128)} %bitcast.42, ...), custom_call_target="tpu_custom_call" | custom-call | flops 2400000000 | bytes 12000000 | tf_op jit(solution)/shard_map/bucket_round/pallas_call | solution.py:240
  7.9 8.4 %collective-permute-start = (f32[2048,256]{1,0:T(8,128)}, f32[2048,256]{1,0:T(8,128)}, u32[]{:S(2)}, u32[]{:S(2)}) collective-permute-start(f32[2048,256]{1,0:T(8,128)} %get-tuple-element.35), channel_id=1, source_target_pairs={{255,0},{0,1},{1,2},{2,3},{3,4},{4,5},{5,6},{6,7},{7,8},{8,9},{9,1... | collective-permute-start | bytes 6291464 | tf_op jit(solution)/shard_map/ppermute | solution.py:485
  16.2 1.3 slice_bitcast_fusion
  17.6 3.8 %collective-permute-start.3 = (f32[16,128]{1,0:T(8,128)S(1)}, f32[16,128]{1,0:T(8,128)S(1)}, u32[]{:S(2)}, u32[]{:S(2)}) collective-permute-start(f32[16,128]{1,0:T(8,128)S(1)} %copy-done.9), channel_id=1, source_target_pairs={{255,0},{0,1},{1,2},{2,3},{3,4},{4,5},{5,6},{6,7},{7,8},{8,9},{9,1... | collective-permute-start | bytes 24584 | tf_op jit(solution)/shard_map/ppermute | solution.py:485
  22.1 0.7 slice_bitcast_fusion.6
  22.8 0.7 slice_bitcast_fusion.4
  23.5 0.7 pad_add_fusion
  24.2 9.8 %collective-permute-done.2 = s32[49]{0:T(128)S(1)} collective-permute-done((s32[49]{0:T(128)S(1)}, s32[49]{0:T(128)S(1)}, u32[]{:S(2)}, u32[]{:S(2)}) %collective-permute-start.2) | collective-permute-done | bytes 228 | tf_op jit(solution)/shard_map/ppermute | solution.py:485
  34.1 5.5 %collective-permute-done.right_in = f32[2048,256]{1,0:T(8,128)} collective-permute-done((f32[2048,256]{1,0:T(8,128)}, f32[2048,256]{1,0:T(8,128)}, u32[]{:S(2)}, u32[]{:S(2)}) %collective-permute-start) | collective-permute-done | bytes 2097184 | tf_op jit(solution)/shard_map/ppermute | solution.py:485
  40.1 9.4 %bucket_round.5 = (f32[2048,256]{1,0:T(8,128)}, f32[16,128]{1,0:T(8,128)}, f32[2048,256]{1,0:T(8,128)}, f32[16,128]{1,0:T(8,128)}, f32[4,256,256]{2,1,0:T(8,128)}) custom-call(s32[4,16]{1,0:T(4,128)} %bitcast.40, s32[4,16]{1,0:T(4,128)} %bitcast.37, s32[4,16]{1,0:T(4,128)} %bitcast.34, s32[4]{0:T(128)} %bitcast.47, f32[16,128]{1,0:T(8,128)} %get-tuple-element.37.lstate, ...), custom_call_target="tpu_custom_call" | custom-call | flops 2400000000 | bytes 12000000 | tf_op jit(solution)/shard_map/bucket_round/pallas_call | solution.py:240
  49.6 2.8 %collective-permute-start.5 = (f32[2048,256]{1,0:T(8,128)}, f32[2048,256]{1,0:T(8,128)}, u32[]{:S(2)}, u32[]{:S(2)}) collective-permute-start(f32[2048,256]{1,0:T(8,128)} %get-tuple-element.45), channel_id=1, source_target_pairs={{255,0},{0,1},{1,2},{2,3},{3,4},{4,5},{5,6},{6,7},{7,8},{8,9},{9,1... | collective-permute-start | bytes 6291464 | tf_op jit(solution)/shard_map/ppermute | solution.py:485
  52.4 9.5 %collective-permute-start.4 = (f32[16,128]{1,0:T(8,128)}, f32[16,128]{1,0:T(8,128)S(1)}, u32[]{:S(2)}, u32[]{:S(2)}) collective-permute-start(f32[16,128]{1,0:T(8,128)} %get-tuple-element.43), channel_id=1, source_target_pairs={{255,0},{0,1},{1,2},{2,3},{3,4},{4,5},{5,6},{6,7},{7,8},{8,9},{9,1... | collective-permute-start | bytes 24584 | tf_op jit(solution)/shard_map/ppermute | solution.py:485
  61.9 13.8 %collective-permute-done.4.rstate = f32[16,128]{1,0:T(8,128)S(1)} collective-permute-done((f32[16,128]{1,0:T(8,128)}, f32[16,128]{1,0:T(8,128)S(1)}, u32[]{:S(2)}, u32[]{:S(2)}) %collective-permute-start.4) | collective-permute-done | bytes 8224 | tf_op jit(solution)/shard_map/ppermute | solution.py:485
  76.3 11.1 %bucket_round.6 = (f32[2048,256]{1,0:T(8,128)}, f32[16,128]{1,0:T(8,128)}, f32[2048,256]{1,0:T(8,128)}, f32[16,128]{1,0:T(8,128)}, f32[4,256,256]{2,1,0:T(8,128)}) custom-call(s32[4,16]{1,0:T(4,128)} %bitcast.41, s32[4,16]{1,0:T(4,128)} %bitcast.38, s32[4,16]{1,0:T(4,128)} %bitcast.35, s32[4]{0:T(128)} %bitcast.48, f32[16,128]{1,0:T(8,128)} %get-tuple-element.42.lstate, ...), custom_call_target="tpu_custom_call" | custom-call | flops 2400000000 | bytes 12000000 | tf_op jit(solution)/shard_map/bucket_round/pallas_call | solution.py:240
  87.5 0.6 reshape.63.rel_state
  88.1 0.7 slice_bitcast_fusion.1
  89.4 28.6 %collective-permute-done.6.lstate = f32[16,128]{1,0:T(8,128)S(1)} collective-permute-done((f32[16,128]{1,0:T(8,128)}, f32[16,128]{1,0:T(8,128)S(1)}, u32[]{:S(2)}, u32[]{:S(2)}) %collective-permute-start.6) | collective-permute-done | bytes 8224 | tf_op jit(solution)/shard_map/ppermute | solution.py:485
  118.6 8.1 %bucket_round.7 = (f32[2048,256]{1,0:T(8,128)}, f32[16,128]{1,0:T(8,128)}, f32[2048,256]{1,0:T(8,128)}, f32[16,128]{1,0:T(8,128)}, f32[4,256,256]{2,1,0:T(8,128)}) custom-call(s32[1,16]{1,0:T(1,128)} %get-tuple-element.66.lefts, s32[1,16]{1,0:T(1,128)} %get-tuple-element.65.rights, s32[1,16]{1,0:T(1,128)} %get-tuple-element.64.kinds, s32[1]{0:T(128)} %slice.46.counts, ...), custom_call_target="tpu_custom_call" | custom-call | flops 2400000000 | bytes 12000000 | tf_op jit(solution)/shard_map/bucket_round/pallas_call | solution.py:240
  126.7 103.8 %bring_home.1 = (f32[2048,256]{1,0:T(8,128)}, f32[16,128]{1,0:T(8,128)}, f32[2048,256]{1,0:T(8,128)}, f32[16,128]{1,0:T(8,128)}, f32[1024,256]{1,0:T(8,128)}, /*index=5*/f32[8,128]{1,0:T(8,128)}) custom-call(f32[2048,256]{1,0:T(8,128)} %get-tuple-element.53.left, f32[16,128]{1,0:T(8,128)} %get-tuple-element.54.lstate, f32[2048,256]{1,0:T(8,128)} %get-tuple-element.55.right, ...), custom_call_target="tpu_custom_call" | custom-call | flops 2000000 | bytes 12000000 | tf_op jit(solution)/shard_map/bring_home/pallas_call | solution.py:448
  230.5 1.3 reshape.67
  231.7 3.2 %copy.22 = f32[2048,256]{1,0:T(8,128)} copy(f32[2048,256]{1,0:T(8,128)} %get-tuple-element.75) | data formatting | bytes 4194304
  234.9 0.6 copy.23
  235.5 1.3 copy.24
  237.5 1.0 copy.26
  (33 shorter events, 3.9 us)
Async XLA Ops:
  7.8 9.8 %copy-start.9 = (f32[16,128]{1,0:T(8,128)S(1)}, f32[16,128]{1,0:T(8,128)}, u32[]{:S(2)}) copy-start(f32[16,128]{1,0:T(8,128)} %get-tuple-element.38) | copy-start | bytes 24580
  7.9 13.6 %copy-start.6 = (s32[1,4]{1,0:T(1,128)S(1)}, s32[1,4]{1,0:T(1,128)}, u32[]{:S(2)}) copy-start(s32[1,4]{1,0:T(1,128)} %param.21) | copy-start | bytes 52
  7.9 31.7 %collective-permute-start = (f32[2048,256]{1,0:T(8,128)}, f32[2048,256]{1,0:T(8,128)}, u32[]{:S(2)}, u32[]{:S(2)}) collective-permute-start(f32[2048,256]{1,0:T(8,128)} %get-tuple-element.35), channel_id=1, source_target_pairs={{255,0},{0,1},{1,2},{2,3},{3,4},{4,5},{5,6},{6,7},{7,8},{8,9},{9,1... | collective-permute-start | bytes 6291464 | tf_op jit(solution)/shard_map/ppermute | solution.py:485
  17.5 16.5 %collective-permute-start.1 = (s32[1,16,128,128]{3,2,1,0:T(8,128)S(1)}, s32[1,16,128,128]{3,2,1,0:T(8,128)S(1)}, u32[]{:S(2)}, u32[]{:S(2)}) collective-permute-start(s32[1,16,128,128]{3,2,1,0:T(8,128)S(1)} %slice_bitcast_fusion), channel_id=1, source_target_pairs={{1,0},{2,1},{3,2},{4,3},{5,4},{6,5},{7,6},{8,7},{9,8},{10,9},{11,1... | collective-permute-start | bytes 3145736 | tf_op jit(solution)/shard_map/ppermute | solution.py:485
  17.6 21.9 %collective-permute-start.3 = (f32[16,128]{1,0:T(8,128)S(1)}, f32[16,128]{1,0:T(8,128)S(1)}, u32[]{:S(2)}, u32[]{:S(2)}) collective-permute-start(f32[16,128]{1,0:T(8,128)S(1)} %copy-done.9), channel_id=1, source_target_pairs={{255,0},{0,1},{1,2},{2,3},{3,4},{4,5},{5,6},{6,7},{7,8},{8,9},{9,1... | collective-permute-start | bytes 24584 | tf_op jit(solution)/shard_map/ppermute | solution.py:485
  24.2 9.9 %collective-permute-start.2 = (s32[49]{0:T(128)S(1)}, s32[49]{0:T(128)S(1)}, u32[]{:S(2)}, u32[]{:S(2)}) collective-permute-start(s32[49]{0:T(128)S(1)} %pad_add_fusion), channel_id=1, source_target_pairs={{1,0},{2,1},{3,2},{4,3},{5,4},{6,5},{7,6},{8,7},{9,8},{10,9},{11,1... | collective-permute-start | bytes 596 | tf_op jit(solution)/shard_map/ppermute | solution.py:485
  34.0 53.4 %copy-start.8 = (s32[1,16,128,128]{3,2,1,0:T(8,128)}, s32[1,16,128,128]{3,2,1,0:T(8,128)S(1)}, u32[]{:S(2)}) copy-start(s32[1,16,128,128]{3,2,1,0:T(8,128)S(1)} %collective-permute-done.1.edges) | copy-start | bytes 3145732
  39.5 0.6 copy-start.4
  49.6 26.1 %collective-permute-start.5 = (f32[2048,256]{1,0:T(8,128)}, f32[2048,256]{1,0:T(8,128)}, u32[]{:S(2)}, u32[]{:S(2)}) collective-permute-start(f32[2048,256]{1,0:T(8,128)} %get-tuple-element.45), channel_id=1, source_target_pairs={{255,0},{0,1},{1,2},{2,3},{3,4},{4,5},{5,6},{6,7},{7,8},{8,9},{9,1... | collective-permute-start | bytes 6291464 | tf_op jit(solution)/shard_map/ppermute | solution.py:485
  52.4 23.3 %collective-permute-start.4 = (f32[16,128]{1,0:T(8,128)}, f32[16,128]{1,0:T(8,128)S(1)}, u32[]{:S(2)}, u32[]{:S(2)}) collective-permute-start(f32[16,128]{1,0:T(8,128)} %get-tuple-element.43), channel_id=1, source_target_pairs={{255,0},{0,1},{1,2},{2,3},{3,4},{4,5},{5,6},{6,7},{7,8},{8,9},{9,1... | collective-permute-start | bytes 24584 | tf_op jit(solution)/shard_map/ppermute | solution.py:485
  75.7 0.6 copy-start.5
  76.3 11.2 %copy-start.7 = (f32[4,256]{1,0:T(4,128)S(1)}, f32[4,256]{1,0:T(4,128)}, u32[]{:S(2)}) copy-start(f32[4,256]{1,0:T(4,128)} %param.16) | copy-start | bytes 12292
  87.4 30.6 %collective-permute-start.7 = (f32[2048,256]{1,0:T(8,128)}, f32[2048,256]{1,0:T(8,128)}, u32[]{:S(2)}, u32[]{:S(2)}) collective-permute-start(f32[2048,256]{1,0:T(8,128)} %get-tuple-element.49), channel_id=1, source_target_pairs={{1,0},{2,1},{3,2},{4,3},{5,4},{6,5},{7,6},{8,7},{9,8},{10,9},{11,1... | collective-permute-start | bytes 6291464 | tf_op jit(solution)/shard_map/ppermute | solution.py:485
  88.1 29.9 %collective-permute-start.6 = (f32[16,128]{1,0:T(8,128)}, f32[16,128]{1,0:T(8,128)S(1)}, u32[]{:S(2)}, u32[]{:S(2)}) collective-permute-start(f32[16,128]{1,0:T(8,128)} %get-tuple-element.47), channel_id=1, source_target_pairs={{1,0},{2,1},{3,2},{4,3},{5,4},{6,5},{7,6},{8,7},{9,8},{10,9},{11,1... | collective-permute-start | bytes 24584 | tf_op jit(solution)/shard_map/ppermute | solution.py:485
  118.0 0.6 copy-start.10
  231.7 3.2 %copy-start.3 = (f32[16,128]{1,0:T(8,128)S(1)}, f32[16,128]{1,0:T(8,128)}, u32[]{:S(2)}) copy-start(f32[16,128]{1,0:T(8,128)} %get-tuple-element.59) | copy-start | bytes 24580
  231.7 3.8 %copy-start = (f32[2048,256]{1,0:T(8,128)S(1)}, f32[2048,256]{1,0:T(8,128)}, u32[]{:S(2)}) copy-start(f32[2048,256]{1,0:T(8,128)} %get-tuple-element.77) | copy-start | bytes 6291460
  235.5 1.3 copy-start.2
  235.5 2.0 copy-start.1
